TPU v7x, 256 devices: a whole 4x4x8 slice. The times are simulated.
256 devices in a mesh: req: 32 (over x, y, core), head: 8 (over z).
Axes of the slice: x: 4, y: 4, z: 8, core: 2. Of those that a mesh axis runs over, the one named last changes fastest.
Arguments:
- hidden_in: bfloat16 [8192, 4096], P('req', 'head'), may hold values from -6 to 6
- norm_gain: float32 [4096], replicated, may hold values from 0.25 to 1.75
- norm_shift: float32 [4096], replicated, may hold values from -3 to 3
- attend_weight: bfloat16 [4096, 3, 2048], P(None, None, 'head'), may hold values from -0.09375 to 0.09375
- output_weight: bfloat16 [2048, 4096], P('head'), may hold values from -0.125 to 0.125
- up_weight: bfloat16 [4096, 8192], P('req', 'head'), may hold values from -0.09375 to 0.09375
- up_bias: float32 [8192], P('head'), may hold values from -3 to 3
- down_weight: bfloat16 [8192, 4096], P('head', 'req'), may hold values from -0.0625 to 0.0625
- down_bias: float32 [4096], P('head'), may hold values from -3 to 3
- key_cache: bfloat16 [64, 1536, 2048], P('req', None, 'head'), may hold values from -160 to 160
- value_cache: bfloat16 [64, 1536, 2048], P('req', None, 'head'), may hold values from -5 to 5
- cached_len: int32 [64], P('req'), may hold values from 1 to 1536, as said below
Outputs:
- hidden_out: bfloat16 [8192, 4096], P('req', 'head')
- new_keys: bfloat16 [64, 128, 2048], P('req', None, 'head')
- new_values: bfloat16 [64, 128, 2048], P('req', None, 'head')
Inputs may be any that keep to these rules, and one draw needn't show every extreme that they name: `cached_len`: each cached length is under 64 or between 768 and 1536; some request has exactly 1536.
All inputs are finite; a program needn't handle non-finite values.
Results may differ from a plain program's by a relative error of at most 0.012.
Values may be sent and summed in bfloat16 or wider, within the bound.
A program may use at most 128 MiB of HBM per device.

v0:
```python
import jax
import jax.numpy as jnp
from jax import lax
from jax.sharding import PartitionSpec as P

HD = 256
ROT = 64
GROUP = 128
BLOCK = 128


epsilon = 1e-05
very_low = -1e30


def layer_norm(values, gain_vec, shift_vec):
    floats = values.astype(jnp.float32)
    center = floats - jnp.mean(floats, axis=-1, keepdims=True)
    spread = jnp.mean(center * center, axis=-1, keepdims=True)
    return center * lax.rsqrt(spread + epsilon) * gain_vec + shift_vec


def rotate_pairs(tensor, positions):
    halves = ROT // 2
    frequency = 10000.0 ** (-(jnp.arange(halves, dtype=jnp.float32) * 2.0) / ROT)
    angles = positions.astype(jnp.float32)[:, :, None] * frequency
    cosine = jnp.cos(angles)[:, :, None, :]
    sine_part = jnp.sin(angles)[:, :, None, :]
    rotary = tensor[..., :ROT]
    even_part = rotary[..., 0::2]
    odd_part = rotary[..., 1::2]
    rotated = jnp.stack(
        [even_part * cosine - odd_part * sine_part, odd_part * cosine + even_part * sine_part],
        axis=-1,
    )
    return jnp.concatenate([rotated.reshape(rotary.shape), tensor[..., ROT:]], axis=-1)


def block_part(query_rows, key_rows, value_rows, lengths, offset):
    batch_size, group_len, head_count, head_size = query_rows.shape
    span_len = key_rows.shape[1]
    keys_four = key_rows.reshape(batch_size, span_len, head_count, head_size)
    values_four = value_rows.reshape(batch_size, span_len, head_count, head_size)
    score_scale = head_size ** (-0.5)
    live_len = jnp.clip(jnp.max(lengths) - offset, 0, span_len)
    steps_count = (live_len + BLOCK - 1) // BLOCK
    start_state = (
        jnp.full((batch_size, head_count, group_len), very_low, jnp.float32),
        jnp.zeros((batch_size, head_count, group_len), jnp.float32),
        jnp.zeros((batch_size, head_count, group_len, head_size), jnp.float32),
    )

    def visit(block_index, carry_state):
        top_score, weight_sum, weighted = carry_state
        block_start = block_index * BLOCK
        key_block = lax.dynamic_slice_in_dim(keys_four, block_start, BLOCK, 1)
        value_block = lax.dynamic_slice_in_dim(values_four, block_start, BLOCK, 1)
        scores = (
            jnp.einsum("rchd,rkhd->rhck", query_rows, key_block, preferred_element_type=jnp.float32)
            * score_scale
        )
        slot_place = offset + block_start + jnp.arange(BLOCK, dtype=jnp.int32)
        visible = (slot_place[None, :] < lengths[:, None])[:, None, None, :]
        scores = jnp.where(visible, scores, very_low)
        new_top = jnp.maximum(top_score, jnp.max(scores, axis=-1))
        rescale = jnp.exp(top_score - new_top)
        weights = jnp.where(visible, jnp.exp(scores - new_top[..., None]), 0.0)
        weight_sum = weight_sum * rescale + jnp.sum(weights, axis=-1)
        weighted = weighted * rescale[..., None] + jnp.einsum(
            "rhck,rkhd->rhcd",
            weights.astype(jnp.bfloat16),
            value_block,
            preferred_element_type=jnp.float32,
        )
        return (new_top, weight_sum, weighted)

    return lax.fori_loop(0, steps_count, visit, start_state)


def group_part(query_rows, key_rows, value_rows):
    group_len = query_rows.shape[1]
    score_scale = query_rows.shape[3] ** (-0.5)
    scores = (
        jnp.einsum("rchd,rkhd->rhck", query_rows, key_rows, preferred_element_type=jnp.float32)
        * score_scale
    )
    causal = jnp.arange(group_len)[:, None] >= jnp.arange(group_len)[None, :]
    scores = jnp.where(causal, scores, very_low)
    top_score = jnp.max(scores, axis=-1)
    weights = jnp.exp(scores - top_score[..., None])
    weighted = jnp.einsum(
        "rhck,rkhd->rhcd",
        weights.astype(jnp.bfloat16),
        value_rows,
        preferred_element_type=jnp.float32,
    )
    return (top_score, jnp.sum(weights, axis=-1), weighted)


def merge_parts(first_part, second_part):
    top_score = jnp.maximum(first_part[0], second_part[0])
    first_scale = jnp.exp(first_part[0] - top_score)
    second_scale = jnp.exp(second_part[0] - top_score)
    weight_sum = first_part[1] * first_scale + second_part[1] * second_scale
    weighted = first_part[2] * first_scale[..., None] + second_part[2] * second_scale[..., None]
    return (top_score, weight_sum, weighted)


def body(
    hidden_in,
    norm_gain,
    norm_shift,
    attend_weight,
    output_weight,
    up_weight,
    up_bias,
    down_weight,
    down_bias,
    key_cache,
    value_cache,
    cached_len,
):
    gathered = lax.all_gather(hidden_in, "head", axis=1, tiled=True)
    normed = layer_norm(gathered, norm_gain, norm_shift).astype(jnp.bfloat16)
    model_width = gathered.shape[1]
    batch_size = key_cache.shape[0]
    local_width = output_weight.shape[0]
    head_count = local_width // HD
    projected = jnp.dot(
        normed,
        attend_weight.reshape(model_width, 3 * local_width),
        preferred_element_type=jnp.float32,
    )
    projected = projected.reshape(batch_size, GROUP, 3, head_count, HD)
    positions = cached_len[:, None] + jnp.arange(GROUP, dtype=jnp.int32)[None, :]
    query_rows = rotate_pairs(projected[:, :, 0], positions).astype(jnp.bfloat16)
    key_rows = rotate_pairs(projected[:, :, 1], positions).astype(jnp.bfloat16)
    value_rows = projected[:, :, 2].astype(jnp.bfloat16)
    group_state = group_part(query_rows, key_rows, value_rows)
    cached = block_part(query_rows, key_cache, value_cache, cached_len, 0)
    top_score, weight_sum, weighted = merge_parts(group_state, cached)
    context = (
        (weighted / weight_sum[..., None])
        .transpose(0, 2, 1, 3)
        .reshape(batch_size * GROUP, local_width)
        .astype(jnp.bfloat16)
    )
    attended = jnp.dot(context, output_weight, preferred_element_type=jnp.float32)
    upward = jnp.dot(
        normed,
        lax.all_gather(up_weight, "req", axis=0, tiled=True),
        preferred_element_type=jnp.float32,
    )
    active = jax.nn.gelu(upward + up_bias, approximate=True).astype(jnp.bfloat16)
    downward = jnp.dot(
        active,
        lax.all_gather(down_weight, "req", axis=1, tiled=True),
        preferred_element_type=jnp.float32,
    )
    summed = lax.psum_scatter(
        attended.astype(jnp.bfloat16), "head", scatter_dimension=1, tiled=True
    ).astype(jnp.float32) + lax.psum_scatter(
        downward.astype(jnp.bfloat16), "head", scatter_dimension=1, tiled=True
    ).astype(
        jnp.float32
    )
    hidden_out = (hidden_in.astype(jnp.float32) + summed + down_bias).astype(jnp.bfloat16)
    new_keys = key_rows.reshape(batch_size, GROUP, local_width)
    new_values = value_rows.reshape(batch_size, GROUP, local_width)
    return (hidden_out, new_keys, new_values)


def solution(mesh):
    placed = (
        P("req", "head"),
        P(),
        P(),
        P(None, None, "head"),
        P("head", None),
        P("req", "head"),
        P("head"),
        P("head", "req"),
        P("head"),
        P("req", None, "head"),
        P("req", None, "head"),
        P("req"),
    )
    return jax.shard_map(
        body,
        mesh=mesh,
        in_specs=placed,
        out_specs=(P("req", "head"), P("req", None, "head"), P("req", None, "head")),
        check_vma=False,
    )
```

profile of v0, /device:TPU:2, one launch (start us, length us, event | category | flops | bytes accessed | tf_op | source)
XLA Modules:
  0.0 275.4 jit_solution(14929506501255324865)
XLA Ops:
  7.2 0.7 all-gather.4.cloned.1.call-update
  8.0 0.7 all-gather.8.cloned.1.call-update
  8.7 0.7 all-gather.6.cloned.1.call-update
  9.4 1.3 reduce_max.33
  11.4 8.7 %copy.44 = bf16[4096,3,256]{0,2,1:T(8,128)(2,1)} copy(bf16[4096,3,256]{2,0,1:T(8,128)(2,1)} %param.17) | data formatting | bytes 12582912 | tf_op args[3]
  20.2 0.6 iota_compare_fusion
  20.8 32.8 %all-gather.4.cloned.1.call-done = bf16[256,4096]{1,0:T(8,128)(2,1)} async-done(((bf16[256,512]{1,0:T(8,128)(2,1)}), bf16[256,4096]{1,0:T(8,128)(2,1)}) %all-gather.4.cloned.1.call-update) | async-done | bytes 2097168 | tf_op jit(solution)/shard_map/all_gather | solution.py:123
  53.6 2.1 convert_reduce_fusion
  55.8 3.0 %fusion.22 = f32[256]{0:T(256)S(1)} fusion(bf16[256,4096]{1,0:T(8,128)(2,1)} %all-gather.4.cloned.1.call-done, f32[256]{0:T(256)S(1)} %broadcast_multiply_fusion), kind=kLoop, calls=%fused_computation.33 | loop fusion | flops 4194048 | bytes 2099200 | tf_op jit(solution)/shard_map/reduce_sum | solution.py:19
  58.8 1.0 fusion.25
  59.9 1.8 fusion.26
  61.8 0.8 slice.62
  62.6 1.8 slice.38
  64.4 1.8 slice.37
  66.2 1.8 slice.43
  67.9 1.8 slice.42
  69.7 1.5 fusion.56
  71.5 0.7 copy.54
  72.3 1.5 fusion.72
  73.8 0.7 copy.50
  74.6 1.5 copy.51
  76.1 1.5 copy.49
  77.5 1.0 pad_maximum_fusion.2
  78.7 0.9 pad_maximum_fusion.1
  79.8 1.1 fusion.86
  81.0 29.6 %while.14 = (s32[]{:T(128)}, f32[2,1,128]{2,0,1:T(2,128)S(1)}, f32[2,1,128]{2,0,1:T(2,128)S(1)}, f32[2,1,128,256]{3,2,0,1:T(8,128)S(1)}, s32[]{:T(128)}, /*index...) while((s32[]{:T(128)}, f32[2,1,128]{2,0,1:T(2,128)S(1)}, ...), condition=%wide.region_7.8_spmd, body=%wide.region_4.7_spmd.sunk | while | flops 33981572 | bytes 1329351 | solution.py:77
  81.0 0.7 broadcast_compare_fusion.2
  81.7 1.1 fusion.103
  83.0 1.2 fusion.106
  84.3 0.7 broadcast_compare_fusion.2
  85.0 1.1 fusion.103
  86.1 0.1 fusion.105
  86.3 1.2 fusion.106
  87.6 0.7 broadcast_compare_fusion.2
  88.3 1.1 fusion.103
  89.6 1.2 fusion.106
  90.8 0.7 broadcast_compare_fusion.2
  91.6 1.1 fusion.103
  92.7 0.1 fusion.105
  92.8 1.3 fusion.106
  94.1 0.7 broadcast_compare_fusion.2
  94.9 1.1 fusion.103
  96.1 1.2 fusion.106
  97.4 0.7 broadcast_compare_fusion.2
  98.1 1.1 fusion.103
  99.4 1.2 fusion.106
  100.7 0.7 broadcast_compare_fusion.2
  101.4 1.1 fusion.103
  102.7 1.3 fusion.106
  104.0 0.7 broadcast_compare_fusion.2
  104.7 1.1 fusion.103
  106.0 1.2 fusion.106
  107.3 0.7 broadcast_compare_fusion.2
  108.0 1.1 fusion.103
  109.3 1.3 fusion.106
  110.6 0.2 fusion.32
  110.9 2.1 convolution_convert_fusion.1
  113.0 0.2 reduce-scatter.5.cloned.1.call-start
  113.2 5.0 %all-gather.8.cloned.1.call-done = bf16[1024,4096]{1,0:T(8,128)(2,1)} async-done(((bf16[1024,128]{1,0:T(8,128)(2,1)}), bf16[1024,4096]{1,0:T(8,128)(2,1)}) %all-gather.8.cloned.1.call-update) | async-done | bytes 8388624 | tf_op jit(solution)/shard_map/all_gather | solution.py:157
  118.2 60.5 %all-gather.6.cloned.1.call-done = bf16[4096,1024]{1,0:T(8,128)(2,1)} async-done(((bf16[128,1024]{1,0:T(8,128)(2,1)}), bf16[4096,1024]{1,0:T(8,128)(2,1)}) %all-gather.6.cloned.1.call-update) | async-done | bytes 8388624 | tf_op jit(solution)/shard_map/all_gather | solution.py:151
  178.7 12.4 %convolution_convert_fusion = bf16[256,4096]{1,0:T(8,128)(2,1)} fusion(bf16[1024,4096]{1,0:T(8,128)(2,1)} %all-gather.8.cloned.1.call-done, bf16[256,4096]{1,0:T(8,128)(2,1)} %copy-done.3, bf16[4096,1024]{1,0:T(8,128)(2,1)} %all-gather.6.cloned.1.call-done, f32[1024]{0:T(1024)} %param.20), kind=kOutput, calls=%fused_computation.29 | convolution fusion | flops 4298637312 | bytes 20975616 | tf_op jit(solution)/shard_map/dot_general | solution.py:155
  191.2 32.3 %reduce-scatter.3.cloned.1.call-done = bf16[256,512]{1,0:T(8,128)(2,1)} async-done(((bf16[256,4096]{1,0:T(8,128)(2,1)}), bf16[256,512]{1,0:T(8,128)(2,1)}) %reduce-scatter.3.cloned.1.call-update) | async-done | bytes 262160 | tf_op jit(solution)/shard_map/reduce_scatter | solution.py:160
  223.5 43.5 %reduce-scatter.5.cloned.1.call-done = bf16[256,512]{1,0:T(8,128)(2,1)} async-done(((bf16[256,4096]{1,0:T(8,128)(2,1)}), bf16[256,512]{1,0:T(8,128)(2,1)}) %reduce-scatter.5.cloned.1.call-update) | async-done | bytes 262160 | tf_op jit(solution)/shard_map/reduce_scatter | solution.py:162
  267.1 1.8 add_convert_fusion
  (97 shorter events, 2.0 us)
Async XLA Ops:
  7.2 103.7 %copy-start = (bf16[256,4096]{1,0:T(8,128)(2,1)S(1)}, bf16[256,4096]{1,0:T(8,128)(2,1)}, u32[]{:S(2)}) copy-start(bf16[256,4096]{1,0:T(8,128)(2,1)} %param.18) | copy-start | bytes 6291460
  7.2 46.5 %all-gather.4.cloned.1.call-start = ((), (), s32[]{:S(2)}) async-start(), calls=%async_computation.2 | async-start | bytes 2359296 | tf_op jit(solution)/shard_map/all_gather | solution.py:123
  7.9 110.3 %all-gather.8.cloned.1.call-start = ((), (), s32[]{:S(2)}) async-start(), calls=%async_computation.5 | async-start | bytes 8650752 | tf_op jit(solution)/shard_map/all_gather | solution.py:157
  8.7 170.1 %all-gather.6.cloned.1.call-start = ((), (), s32[]{:S(2)}) async-start(), calls=%async_computation.4 | async-start | bytes 8650752 | tf_op jit(solution)/shard_map/all_gather | solution.py:151
  9.4 214.1 %reduce-scatter.3.cloned.1.call-start = ((), (), s32[]{:S(2)}) async-start(), calls=%async_computation.3 | async-start | bytes 2359296 | tf_op jit(solution)/shard_map/reduce_scatter | solution.py:160
  11.4 9.4 %copy-start.13 = (s32[2]{0:T(128)S(1)}, s32[2]{0:T(128)}, u32[]{:S(2)}) copy-start(s32[2]{0:T(128)} %param.25) | copy-start | bytes 28
  20.1 38.7 %copy-start.8 = (f32[4096]{0:T(1024)S(1)}, f32[4096]{0:T(1024)}, u32[]{:S(2)}) copy-start(f32[4096]{0:T(1024)} %param.16) | copy-start | bytes 49156
  20.1 38.7 %copy-start.9 = (f32[4096]{0:T(1024)S(1)}, f32[4096]{0:T(1024)}, u32[]{:S(2)}) copy-start(f32[4096]{0:T(1024)} %param.15) | copy-start | bytes 49156
  20.1 49.6 %copy-start.12 = (f32[32]{0:T(128)}, f32[32]{0:T(128)S(1)}, u32[]{:S(2)}) copy-start(f32[32]{0:T(128)S(1)} %multiply_power_fusion) | copy-start | bytes 388
  20.8 48.9 %copy-start.10 = (f32[2,128]{1,0:T(2,128)}, f32[2,128]{1,0:T(2,128)S(1)}, u32[]{:S(2)}) copy-start(f32[2,128]{1,0:T(2,128)S(1)} %add_convert_fusion.1) | copy-start | bytes 3076
  53.6 5.2 %copy-start.1 = (bf16[256,4096]{1,0:T(8,128)(2,1)S(1)}, bf16[256,4096]{1,0:T(8,128)(2,1)}, u32[]{:S(2)}) copy-start(bf16[256,4096]{1,0:T(8,128)(2,1)} %all-gather.4.cloned.1.call-done) | copy-start | bytes 6291460
  53.6 6.2 %copy-start.2 = (bf16[4096,3,256]{0,2,1:T(8,128)(2,1)S(1)}, bf16[4096,3,256]{0,2,1:T(8,128)(2,1)}, u32[]{:S(2)}) copy-start(bf16[4096,3,256]{0,2,1:T(8,128)(2,1)} %copy.44) | copy-start | bytes 18874372
  59.9 1.9 copy-start.3
  71.5 2.3 copy-start.5
  79.6 31.0 %copy-start.6 = (bf16[2,128,256]{2,1,0:T(8,128)(2,1)}, bf16[2,128,256]{2,1,0:T(8,128)(2,1)S(1)}, u32[]{:S(2)}) copy-start(bf16[2,128,256]{2,1,0:T(8,128)(2,1)S(1)} %pad_maximum_fusion.1) | copy-start | bytes 393220
  110.6 80.5 %copy-start.7 = (bf16[2,128,256]{2,1,0:T(8,128)(2,1)}, bf16[2,128,256]{2,1,0:T(8,128)(2,1)S(1)}, u32[]{:S(2)}) copy-start(bf16[2,128,256]{2,1,0:T(8,128)(2,1)S(1)} %fusion.64) | copy-start | bytes 393220
  113.0 154.1 %copy-start.4 = (bf16[256,512]{1,0:T(8,128)(2,1)S(1)}, bf16[256,512]{1,0:T(8,128)(2,1)}, u32[]{:S(2)}) copy-start(bf16[256,512]{1,0:T(8,128)(2,1)} %param.14) | copy-start | bytes 786436
  113.0 154.1 %copy-start.11 = (f32[512]{0:T(512)S(1)}, f32[512]{0:T(512)}, u32[]{:S(2)}) copy-start(f32[512]{0:T(512)} %param.22) | copy-start | bytes 6148
  113.0 154.1 %reduce-scatter.5.cloned.1.call-start = ((), (), s32[]{:S(2)}) async-start(), calls=%async_computation.6 | async-start | bytes 2359296 | tf_op jit(solution)/shard_map/reduce_scatter | solution.py:162
Sparse Core Ops, SparseCore 0:
  9.8 43.8 all-gather.3
  56.1 62.0 all-gather.7
  120.8 57.8 all-gather.5
  181.1 42.3 reduce-scatter.2
  225.9 41.0 reduce-scatter.4
where the time goes:
time: 277 us; the launch traced here: 275 us
  waiting for transfers between devices  176 us (64%)
  matrix products  38.9 us (14%)
  other arithmetic  23 us (8%)
  local copies, waits for them, and re-layouts  21.6 us (8%)
  between operations  14.7 us (5%)
    all_gather x1, waiting for transfers between devices, body(): lax.all_gather(up_weight, 'req', axis=0, tiled=True)  60.5 us
    reduce_scatter x1, waiting for transfers between devices, body(): lax.psum_scatter(downward.astype(jnp.bfloat16), 'head', scatter_dimension...  43.5 us
    all_gather x1, waiting for transfers between devices, body(): gathered = lax.all_gather(hidden_in, 'head', axis=1, tiled=True)  32.8 us
    reduce_scatter x1, waiting for transfers between devices, body(): lax.psum_scatter(attended.astype(jnp.bfloat16), 'head', scatter_dimension...  32.3 us
    dot_general x1, matrix products, body(): jnp.dot(active, lax.all_gather(down_weight, 'req', axis=1, tiled=True), p...  12.4 us
    dot_general x9, matrix products, visit(): jnp.einsum('rhck,rkhd->rhcd', weights.astype(jnp.bfloat16), value_block,...  11.2 us
    dot_general x9, matrix products, visit(): jnp.einsum('rchd,rkhd->rhck', query_rows, key_block, preferred_element_ty...  10 us
    unnamed x29, local copies, waits for them, and re-layouts  8.79 us
  transfers between devices with their start and end apart: 5, of which 5 were waited for; matrix products, arithmetic and copies ran while one was open for 30% of the time, Pallas kernels for 0%

commit v1 on v0

v1 whole, which is shorter than its diff:
```python
import functools

import jax
import jax.numpy as jnp
import numpy as np
from jax import lax
from jax.experimental import pallas as pl
from jax.experimental.pallas import tpu as pltpu
from jax.sharding import PartitionSpec as P

HD = 256
ROT = 64
GROUP = 128
D = 4096
TOK = 256
UNITS = 1024
SLOTS = 1536
Z = 8
COLS = D // Z
epsilon = 1e-05
very_low = -1e30
MESH = pl.DeviceIdType.MESH
F32 = jnp.float32
BF16 = jnp.bfloat16


def kernel(
    hid, gain, shift, wq, wo, wu, ub, wd, db, kc, vc, freq, lens,
    out, new_k, new_v,
    xg, nrm, wub, wdb, wqv, wov, kcv, vcv, gainv, shiftv, ubv, dbv, freqv,
    qbuf, kbuf, vbuf, ctx, act, part, rsend, rrecv,
    local_sem, zs, zr, ws, wr, ss, sr,
):
    r = lax.axis_index("req")
    z = lax.axis_index("head")
    core = r % 2
    y = (r // 2) % 4
    x = r // 8

    def device(c, a_, b_):
        x_ = (1 - c) * a_ + c * b_
        y_ = (1 - c) * b_ + c * a_
        return ((x_ % 4) * 4 + (y_ % 4)) * 2 + c

    a = (1 - core) * x + core * y
    b = (1 - core) * y + core * x
    partner = device(1 - core, b, a)
    a_plus, a_minus = device(core, a + 1, b), device(core, a + 3, b)
    b_plus, b_minus = device(core, a, b + 1), device(core, a, b + 3)
    z_plus, z_minus = (z + 1) % Z, (z + 7) % Z

    barrier = pltpu.get_barrier_semaphore()
    for who in (
        (a_plus, z), (a_minus, z), (b_plus, z), (b_minus, z), (partner, z),
        (r, z_plus), (r, z_minus),
    ):
        pl.semaphore_signal(barrier, inc=1, device_id=who, device_id_type=MESH)
    pl.semaphore_wait(barrier, 7)

    sent = []

    def remote(src, dst, send, recv, who):
        return pltpu.make_async_remote_copy(
            src_ref=src, dst_ref=dst, send_sem=send, recv_sem=recv,
            device_id=who, device_id_type=MESH,
        )

    def launch(src, dst, send, recv, who):
        copy = remote(src, dst, send, recv, who)
        copy.start()
        sent.append(copy)

    def zchunk(origin, c):
        return xg.at[origin, pl.ds(128 * c, 128), :]

    def zindex(direction, hop, c):
        return direction * 8 + (hop - 1) * 2 + c

    def zsend(direction, hop, c):
        origin = (z + Z - (hop - 1)) % Z if direction == 0 else (z + hop - 1) % Z
        src = hid.at[pl.ds(128 * c, 128), :] if hop == 1 else zchunk(origin, c)
        k = zindex(direction, hop, c)
        launch(src, zchunk(origin, c), zs.at[k], zr.at[k], (r, z_plus if direction == 0 else z_minus))

    def zwait(direction, hop, c):
        origin = (z + Z - hop) % Z if direction == 0 else (z + hop) % Z
        k = zindex(direction, hop, c)
        view = zchunk(origin, c)
        remote(view, view, zs.at[k], zr.at[k], (r, z_plus)).wait_recv()

    def zlast(direction, c):
        return 4 if c == direction else 3

    def zevent(direction, hop, c):
        zwait(direction, hop, c)
        if hop < zlast(direction, c):
            zsend(direction, hop + 1, c)

    own = (wu, wd)

    def slot(w, o):
        if w == 0:
            return wub.at[pl.ds(pl.multiple_of(o * 128, 128), 128), :]
        return wdb.at[o]

    def half(w, o, k):
        if w == 0:
            return wub.at[pl.ds(pl.multiple_of(o * 128 + 64 * k, 64), 64), :]
        return wdb.at[o, pl.ds(512 * k, 512), :]

    A_OF = (0, 3, 1, 2)

    def wsend(w, k, src, dst, who):
        launch(src, dst, ws.at[w, k], wr.at[w, k], (who, z))

    def wwait(w, k, view):
        remote(view, view, ws.at[w, k], wr.at[w, k], (partner, z)).wait_recv()

    def across(w, j, kb):
        o = device(core, a + A_OF[j], b + A_OF[kb])
        src = own[w] if j == 0 and kb == 0 else slot(w, o)
        wsend(w, 20 + 4 * j + kb, src, slot(w, o), partner)

    def second(w, j):
        o = device(core, a + A_OF[j], b)
        src = own[w] if j == 0 else slot(w, o)
        wsend(w, 4 + 4 * j, src, slot(w, o), b_plus)
        wsend(w, 5 + 4 * j, src, slot(w, o), b_minus)

    def start_own(w):
        wsend(w, 0, own[w], slot(w, r), a_plus)
        wsend(w, 1, own[w], slot(w, r), a_minus)
        second(w, 0)
        across(w, 0, 0)

    def first_event(w):
        o = device(core, a + 3, b)
        wwait(w, 0, slot(w, o))
        wsend(w, 2, half(w, o, 0), half(w, o, 0), a_plus)
        o = device(core, a + 1, b)
        wwait(w, 1, slot(w, o))
        wsend(w, 3, half(w, o, 1), half(w, o, 1), a_minus)
        second(w, 1)
        second(w, 2)
        across(w, 1, 0)
        across(w, 2, 0)

    def first_halves(w):
        o = device(core, a + 2, b)
        wwait(w, 2, half(w, o, 0))
        wwait(w, 3, half(w, o, 1))
        second(w, 3)
        across(w, 3, 0)

    def second_event(w, j):
        aj = a + A_OF[j]
        o = device(core, aj, b + 3)
        wwait(w, 4 + 4 * j, slot(w, o))
        wsend(w, 6 + 4 * j, half(w, o, 0), half(w, o, 0), b_plus)
        o = device(core, aj, b + 1)
        wwait(w, 5 + 4 * j, slot(w, o))
        wsend(w, 7 + 4 * j, half(w, o, 1), half(w, o, 1), b_minus)
        across(w, j, 1)
        across(w, j, 2)

    def second_halves(w, j):
        o = device(core, a + A_OF[j], b + 2)
        wwait(w, 6 + 4 * j, half(w, o, 0))
        wwait(w, 7 + 4 * j, half(w, o, 1))
        across(w, j, 3)

    def partner_waits(w):
        for j in range(4):
            for kb in range(4):
                o = device(1 - core, b + A_OF[j], a + A_OF[kb])
                wwait(w, 20 + 4 * j + kb, slot(w, o))

    locals_ = []

    def bring(src, dst):
        copy = pltpu.make_async_copy(src, dst, local_sem.at[len(locals_)])
        copy.start()
        locals_.append(copy)
        return copy

    for c in range(2):
        zsend(0, 1, c)
        zsend(1, 1, c)
    start_own(0)
    start_own(1)
    c_x = bring(hid, xg.at[z])
    c_small = [bring(gain, gainv), bring(shift, shiftv), bring(ub, ubv), bring(db, dbv), bring(freq, freqv)]
    c_u = bring(wu, slot(0, r))
    c_d = bring(wd, slot(1, r))
    c_q = bring(wq, wqv)
    c_k = bring(kc, kcv)
    c_v = bring(vc, vcv)
    c_o = bring(wo, wov)
    for copy in c_small:
        copy.wait()

    lane = lax.broadcasted_iota(jnp.int32, (TOK, 128), 1)
    row = lax.broadcasted_iota(jnp.int32, (TOK, 128), 0)
    position = jnp.where(row < GROUP, lens[0] + row, lens[1] + row - GROUP)
    angle = position.astype(F32) * freqv[...]
    cosine = jnp.cos(angle)
    sine = jnp.sin(angle)
    sine = jnp.where(lane % 2 == 0, -sine, sine)

    def rotate(t):
        head = t[:, :128]
        swapped = jnp.where(lane % 2 == 0, pltpu.roll(head, 127, 1), pltpu.roll(head, 1, 1))
        return jnp.concatenate([head * cosine + swapped * sine, t[:, 128:]], axis=1)

    zevent(0, 1, 0), zevent(1, 1, 0)
    first_event(0)
    second_event(0, 0)
    zevent(0, 1, 1), zevent(1, 1, 1)
    zevent(0, 2, 0), zevent(1, 2, 0)
    zevent(0, 2, 1), zevent(1, 2, 1)
    first_event(1)
    second_event(1, 0)
    zevent(0, 3, 0), zevent(1, 3, 0)
    first_halves(0)
    second_halves(0, 0)
    zevent(0, 3, 1), zevent(1, 3, 1)
    second_event(0, 1)
    second_event(0, 2)
    zevent(0, 4, 0), zevent(1, 4, 1)
    c_x.wait()

    @pl.loop(0, TOK // 16)
    def _(i):
        rows = pl.ds(pl.multiple_of(i * 16, 16), 16)
        total = jnp.zeros((16, 1), F32)
        for h in range(Z):
            total += jnp.sum(xg[h, rows, :].astype(F32), axis=1, keepdims=True)
        mean = total * (1.0 / D)
        square = jnp.zeros((16, 1), F32)
        for h in range(Z):
            center = xg[h, rows, :].astype(F32) - mean
            square += jnp.sum(center * center, axis=1, keepdims=True)
        scale = lax.rsqrt(square * (1.0 / D) + epsilon)
        for h in range(Z):
            cols = slice(h * COLS, (h + 1) * COLS)
            center = xg[h, rows, :].astype(F32) - mean
            nrm[rows, cols] = (center * scale * gainv[:, cols] + shiftv[:, cols]).astype(BF16)

    first_halves(1)
    second_halves(1, 0)
    second_event(0, 3)

    c_q.wait()
    qbuf[...] = rotate(jnp.dot(nrm[...], wqv[0], preferred_element_type=F32)).astype(BF16)
    second_halves(0, 1)
    second_halves(0, 2)
    kbuf[...] = rotate(jnp.dot(nrm[...], wqv[1], preferred_element_type=F32)).astype(BF16)
    vbuf[...] = jnp.dot(nrm[...], wqv[2], preferred_element_type=F32).astype(BF16)
    second_event(1, 1)
    second_event(1, 2)
    second_halves(0, 3)
    for q in range(2):
        new_k[q] = kbuf[pl.ds(q * GROUP, GROUP), :]
        new_v[q] = vbuf[pl.ds(q * GROUP, GROUP), :]

    c_k.wait()
    c_v.wait()
    nt = (((1,), (1,)), ((), ()))

    def attend(q):
        rows = pl.ds(q * GROUP, GROUP)
        query = qbuf[rows, :]
        old = lax.dot_general(query, kcv[q], nt, preferred_element_type=F32) * (HD ** -0.5)
        fresh = lax.dot_general(query, kbuf[rows, :], nt, preferred_element_type=F32) * (HD ** -0.5)
        place = lax.broadcasted_iota(jnp.int32, (GROUP, SLOTS), 1)
        old = jnp.where(place < lens[q], old, very_low)
        i0 = lax.broadcasted_iota(jnp.int32, (GROUP, GROUP), 0)
        i1 = lax.broadcasted_iota(jnp.int32, (GROUP, GROUP), 1)
        fresh = jnp.where(i1 <= i0, fresh, very_low)
        top = jnp.maximum(jnp.max(old, axis=1, keepdims=True), jnp.max(fresh, axis=1, keepdims=True))
        old = jnp.exp(old - top)
        fresh = jnp.exp(fresh - top)
        total = jnp.sum(old, axis=1, keepdims=True) + jnp.sum(fresh, axis=1, keepdims=True)
        mixed = jnp.dot(old.astype(BF16), vcv[q], preferred_element_type=F32)
        mixed += jnp.dot(fresh.astype(BF16), vbuf[rows, :], preferred_element_type=F32)
        ctx[rows, :] = (mixed / total).astype(BF16)

    attend(0)
    second_event(1, 3)
    attend(1)

    c_u.wait()
    partner_waits(0)

    @pl.loop(0, UNITS // 256)
    def _(n):
        cols = pl.ds(pl.multiple_of(n * 256, 256), 256)
        upward = jnp.dot(nrm[...], wub[:, cols], preferred_element_type=F32) + ubv[:, cols]
        act[:, cols] = jax.nn.gelu(upward, approximate=True).astype(BF16)

    second_halves(1, 1)
    second_halves(1, 2)
    second_halves(1, 3)
    c_d.wait()
    c_o.wait()
    partner_waits(1)

    def block(t):
        for i in range(2):
            weight = jnp.concatenate([wdb[4 * t + 2 * i], wdb[4 * t + 2 * i + 1]], axis=1)
            cols = pl.ds(pl.multiple_of(t * COLS + 256 * i, 256), 256)
            part[t, :, 256 * i:256 * (i + 1)] = jnp.dot(
                act[...], weight, preferred_element_type=F32
            ) + jnp.dot(ctx[...], wov[:, cols], preferred_element_type=F32)

    def rwait(direction, s, c):
        k = direction * 14 + 2 * s + c
        view = rrecv.at[direction, s, pl.ds(64 * c, 64), :]
        remote(view, view, ss.at[k], sr.at[k], (r, z_plus)).wait_recv()

    block((z + 7) % Z)
    for s in range(7):
        for direction in range(2):
            if s < 3 and direction == 1:
                block((z + 1 + s) % Z)
            t = (z + 7 - s) % Z if direction == 0 else (z + 1 + s) % Z
            for c in range(2):
                rows = pl.ds(128 * direction + 64 * c, 64)
                inner = pl.ds(64 * c, 64)
                value = part[t, rows, :]
                if s > 0:
                    rwait(direction, s - 1, c)
                    value += rrecv[direction, s - 1, inner, :].astype(F32)
                rsend[direction, s, inner, :] = value.astype(BF16)
                k = direction * 14 + 2 * s + c
                launch(
                    rsend.at[direction, s, inner, :], rrecv.at[direction, s, inner, :],
                    ss.at[k], sr.at[k], (r, z_plus if direction == 0 else z_minus),
                )
        if s < 3:
            block((z + 6 - s) % Z)
        if s == 3:
            block(z)
    for direction in range(2):
        for c in range(2):
            rows = pl.ds(128 * direction + 64 * c, 64)
            inner = pl.ds(64 * c, 64)
            rwait(direction, 6, c)
            value = part[z, rows, :] + rrecv[direction, 6, inner, :].astype(F32)
            out[rows, :] = (xg[z, rows, :].astype(F32) + value + dbv[...]).astype(BF16)
    for copy in sent:
        copy.wait_send()


def body(
    hidden_in, norm_gain, norm_shift, attend_weight, output_weight, up_weight,
    up_bias, down_weight, down_bias, key_cache, value_cache, cached_len,
):
    lanes = np.arange(128)
    freq = np.where(lanes < ROT, 10000.0 ** (-(2.0 * (lanes // 2)) / ROT), 0.0)
    freq = jnp.asarray(freq[None, :], dtype=F32)
    anywhere = pl.BlockSpec(memory_space=pl.ANY)
    vmem = pl.BlockSpec(memory_space=pltpu.VMEM)
    dma = pltpu.SemaphoreType.DMA
    return pl.pallas_call(
        kernel,
        out_shape=(
            jax.ShapeDtypeStruct((TOK, COLS), BF16),
            jax.ShapeDtypeStruct((2, GROUP, HD), BF16),
            jax.ShapeDtypeStruct((2, GROUP, HD), BF16),
        ),
        in_specs=[anywhere] * 12 + [pl.BlockSpec(memory_space=pltpu.SMEM)],
        out_specs=(vmem, vmem, vmem),
        scratch_shapes=[
            pltpu.VMEM((Z, TOK, COLS), BF16),
            pltpu.VMEM((TOK, D), BF16),
            pltpu.VMEM((D, UNITS), BF16),
            pltpu.VMEM((32, UNITS, 128), BF16),
            pltpu.VMEM((3, D, HD), BF16),
            pltpu.VMEM((HD, D), BF16),
            pltpu.VMEM((2, SLOTS, HD), BF16),
            pltpu.VMEM((2, SLOTS, HD), BF16),
            pltpu.VMEM((1, D), F32),
            pltpu.VMEM((1, D), F32),
            pltpu.VMEM((1, UNITS), F32),
            pltpu.VMEM((1, COLS), F32),
            pltpu.VMEM((1, 128), F32),
            pltpu.VMEM((TOK, HD), BF16),
            pltpu.VMEM((TOK, HD), BF16),
            pltpu.VMEM((TOK, HD), BF16),
            pltpu.VMEM((TOK, HD), BF16),
            pltpu.VMEM((TOK, UNITS), BF16),
            pltpu.VMEM((Z, TOK, COLS), F32),
            pltpu.VMEM((2, 7, 128, COLS), BF16),
            pltpu.VMEM((2, 7, 128, COLS), BF16),
            dma((12,)),
            dma((16,)),
            dma((16,)),
            dma((2, 36)),
            dma((2, 36)),
            dma((28,)),
            dma((28,)),
        ],
        compiler_params=pltpu.CompilerParams(
            collective_id=0, has_side_effects=True, vmem_limit_bytes=66 * 1000 * 1000
        ),
    )(
        hidden_in, norm_gain[None, :], norm_shift[None, :],
        jnp.transpose(attend_weight, (1, 0, 2)), output_weight, up_weight,
        up_bias[None, :], down_weight, down_bias[None, :], key_cache, value_cache, freq, cached_len,
    )


def solution(mesh):
    placed = (
        P("req", "head"), P(), P(), P(None, None, "head"), P("head", None), P("req", "head"),
        P("head"), P("head", "req"), P("head"), P("req", None, "head"), P("req", None, "head"), P("req"),
    )
    return jax.shard_map(
        body,
        mesh=mesh,
        in_specs=placed,
        out_specs=(P("req", "head"), P("req", None, "head"), P("req", None, "head")),
        check_vma=False,
    )
```

time: 277 us -> 94.6 us (0.34)
  waiting for transfers between devices: 176 us -> 0 us
  Pallas kernels: 0 us -> 89 us
  matrix products: 38.9 us -> 0 us
  other arithmetic: 23 us -> 0 us
  local copies, waits for them, and re-layouts: 21.6 us -> 4.8 us
  between operations: 14.7 us -> 0.64 us
    all_gather x3 -> x0, waiting for transfers between devices: 98.3 us -> none  [the longest x1 60.5 us: body(): lax.all_gather(up_weight, 'req', axis=0, tiled=True)]
    pallas_call x0 -> x1, Pallas kernels: none -> 89 us  [body(): pl.pallas_call(kernel, out_shape=(jax.ShapeDtypeStruct((TOK, COLS), BF16)...]
    reduce_scatter x2 -> x0, waiting for transfers between devices: 75.9 us -> none  [the longest x1 43.5 us: body(): lax.psum_scatter(downward.astype(jnp.bfloat16), 'head', scatter_dimension...]
    dot_general x23 -> x0, matrix products: 38.9 us -> none  [the longest x1 12.4 us: body(): jnp.dot(active, lax.all_gather(down_weight, 'req', axis=1, tiled=True), p...]
    slice x7 -> x0, local copies, waits for them, and re-layouts: 7.91 us -> none  [the longest x2 3.59 us: rotate_pairs(): odd_part = rotary[..., 1::2]]
    lt x9 -> x0, other arithmetic: 6.59 us -> none  [visit(): visible = (slot_place[None, :] < lengths[:, None])[:, None, None, :]]
    reduce_sum x12 -> x0, other arithmetic: 6.22 us -> none  [the longest x1 3.04 us: layer_norm(): spread = jnp.mean(center * center, axis=-1, keepdims=True)]
    unnamed x29 -> x3, local copies, waits for them, and re-layouts: 8.79 us -> 4.8 us
  transfers between devices with their start and end apart: 5 -> 0, of which waited for: 5 -> 0; matrix products, arithmetic and copies ran while one was open for 30% -> 0% of each run, Pallas kernels for 0% -> 0%
where the time goes in v1:
time: 94.6 us; the launch traced here: 94.4 us
  Pallas kernels  89 us (94%)
  local copies, waits for them, and re-layouts  4.8 us (5%)
    pallas_call x1, Pallas kernels, body(): pl.pallas_call(kernel, out_shape=(jax.ShapeDtypeStruct((TOK, COLS), BF16)...  89 us
    unnamed x3, local copies, waits for them, and re-layouts  4.8 us

profile of v1, /device:TPU:2, one launch (start us, length us, event | category | flops | bytes accessed | tf_op | source)
XLA Modules:
  0.0 94.4 jit_solution(1871347041007034098)
XLA Ops:
  0.6 89.0 %shard_map.148 = (bf16[256,512]{1,0:T(8,128)(2,1)}, bf16[2,128,256]{2,1,0:T(8,128)(2,1)}, bf16[2,128,256]{2,1,0:T(8,128)(2,1)}) custom-call(bf16[256,512]{1,0:T(8,128)(2,1)} %hid.1, f32[1,4096]{1,0:T(1,128)} %bitcast.6, f32[1,4096]{1,0:T(1,128)} %bitcast.7, bf16[3,4096,256]{2,1,0:T(8,128)(2,1)} %bitcast.5, bf16[256,4096]{1,0:T(8,128)(2,1)} %wo.1, ...), custom_call_target="tpu_custom_call" | custom-call | tf_op jit(solution)/shard_map/pallas_call | solution.py:365
  89.6 1.7 %copy.19 = bf16[256,512]{1,0:T(8,128)(2,1)} copy(bf16[256,512]{1,0:T(8,128)(2,1)} %get-tuple-element.6) | data formatting | bytes 524288
  91.3 1.6 %copy.20 = bf16[2,128,256]{2,1,0:T(8,128)(2,1)} copy(bf16[2,128,256]{2,1,0:T(8,128)(2,1)} %get-tuple-element.7) | data formatting | bytes 262144
  92.8 1.6 %copy.21 = bf16[2,128,256]{2,1,0:T(8,128)(2,1)} copy(bf16[2,128,256]{2,1,0:T(8,128)(2,1)} %get-tuple-element.8) | data formatting | bytes 262144

commit v2 on v1

--- a/solution.py
+++ b/solution.py
@@ -19,16 +19,17 @@
 COLS = D // Z
 epsilon = 1e-05
 very_low = -1e30
+PIECES = 4
 MESH = pl.DeviceIdType.MESH
 F32 = jnp.float32
 BF16 = jnp.bfloat16
 
 
 def kernel(
-    hid, gain, shift, wq, wo, wu, ub, wd, db, kc, vc, freq, lens,
+    hid, gain, shift, wq, wo, wu, ub, wd, db, kc, vc, freq, lens_in,
     out, new_k, new_v,
     xg, nrm, wub, wdb, wqv, wov, kcv, vcv, gainv, shiftv, ubv, dbv, freqv,
-    qbuf, kbuf, vbuf, ctx, act, part, rsend, rrecv,
+    qbuf, kbuf, vbuf, ctx, act, part, rsend, rrecv, lens,
     local_sem, zs, zr, ws, wr, ss, sr,
 ):
     r = lax.axis_index("req")
@@ -189,7 +190,7 @@
     start_own(0)
     start_own(1)
     c_x = bring(hid, xg.at[z])
-    c_small = [bring(gain, gainv), bring(shift, shiftv), bring(ub, ubv), bring(db, dbv), bring(freq, freqv)]
+    c_small = [bring(lens_in, lens), bring(gain, gainv), bring(shift, shiftv), bring(ub, ubv), bring(db, dbv), bring(freq, freqv)]
     c_u = bring(wu, slot(0, r))
     c_d = bring(wd, slot(1, r))
     c_q = bring(wq, wqv)
@@ -200,12 +201,18 @@
         copy.wait()
 
     lane = lax.broadcasted_iota(jnp.int32, (TOK, 128), 1)
-    row = lax.broadcasted_iota(jnp.int32, (TOK, 128), 0)
-    position = jnp.where(row < GROUP, lens[0] + row, lens[1] + row - GROUP)
-    angle = position.astype(F32) * freqv[...]
-    cosine = jnp.cos(angle)
-    sine = jnp.sin(angle)
-    sine = jnp.where(lane % 2 == 0, -sine, sine)
+    turn = [lens[q].astype(F32) * freqv[pl.ds(0, 8), :] for q in range(2)]
+
+    def rotation():
+        cosines, sines = [], []
+        for q in range(2):
+            cl, sl = jnp.cos(turn[q])[:1], jnp.sin(turn[q])[:1]
+            ct, st = freqv[pl.ds(8, GROUP), :], freqv[pl.ds(8 + GROUP, GROUP), :]
+            cosines.append(cl * ct - sl * st)
+            sines.append(sl * ct + cl * st)
+        cosine = jnp.concatenate(cosines, axis=0)
+        sine = jnp.concatenate(sines, axis=0)
+        return cosine, jnp.where(lane % 2 == 0, -sine, sine)
 
     def rotate(t):
         head = t[:, :128]
@@ -250,6 +257,7 @@
     second_halves(1, 0)
     second_event(0, 3)
 
+    cosine, sine = rotation()
     c_q.wait()
     qbuf[...] = rotate(jnp.dot(nrm[...], wqv[0], preferred_element_type=F32)).astype(BF16)
     second_halves(0, 1)
@@ -313,38 +321,47 @@
                 act[...], weight, preferred_element_type=F32
             ) + jnp.dot(ctx[...], wov[:, cols], preferred_element_type=F32)
 
+    piece = GROUP // PIECES
+
     def rwait(direction, s, c):
-        k = direction * 14 + 2 * s + c
-        view = rrecv.at[direction, s, pl.ds(64 * c, 64), :]
+        k = (direction * 7 + s) * PIECES + c
+        view = rrecv.at[direction, s, pl.ds(piece * c, piece), :]
         remote(view, view, ss.at[k], sr.at[k], (r, z_plus)).wait_recv()
 
+    def hand_on(direction, s):
+        t = (z + 7 - s) % Z if direction == 0 else (z + 1 + s) % Z
+        for c in range(PIECES):
+            rows = pl.ds(128 * direction + piece * c, piece)
+            inner = pl.ds(piece * c, piece)
+            value = part[t, rows, :]
+            if s > 0:
+                rwait(direction, s - 1, c)
+                value += rrecv[direction, s - 1, inner, :].astype(F32)
+            rsend[direction, s, inner, :] = value.astype(BF16)
+            k = (direction * 7 + s) * PIECES + c
+            launch(
+                rsend.at[direction, s, inner, :], rrecv.at[direction, s, inner, :],
+                ss.at[k], sr.at[k], (r, z_plus if direction == 0 else z_minus),
+            )
+
     block((z + 7) % Z)
-    for s in range(7):
+    hand_on(0, 0)
+    block((z + 1) % Z)
+    hand_on(1, 0)
+    for s in range(1, 7):
+        if s < 3:
+            block((z + 7 - s) % Z)
+            block((z + 1 + s) % Z)
+        elif s == 3:
+            block((z + 4) % Z)
+        elif s == 4:
+            block(z)
+        hand_on(0, s)
+        hand_on(1, s)
+    for c in range(PIECES):
         for direction in range(2):
-            if s < 3 and direction == 1:
-                block((z + 1 + s) % Z)
-            t = (z + 7 - s) % Z if direction == 0 else (z + 1 + s) % Z
-            for c in range(2):
-                rows = pl.ds(128 * direction + 64 * c, 64)
-                inner = pl.ds(64 * c, 64)
-                value = part[t, rows, :]
-                if s > 0:
-                    rwait(direction, s - 1, c)
-                    value += rrecv[direction, s - 1, inner, :].astype(F32)
-                rsend[direction, s, inner, :] = value.astype(BF16)
-                k = direction * 14 + 2 * s + c
-                launch(
-                    rsend.at[direction, s, inner, :], rrecv.at[direction, s, inner, :],
-                    ss.at[k], sr.at[k], (r, z_plus if direction == 0 else z_minus),
-                )
-        if s < 3:
-            block((z + 6 - s) % Z)
-        if s == 3:
-            block(z)
-    for direction in range(2):
-        for c in range(2):
-            rows = pl.ds(128 * direction + 64 * c, 64)
-            inner = pl.ds(64 * c, 64)
+            rows = pl.ds(128 * direction + piece * c, piece)
+            inner = pl.ds(piece * c, piece)
             rwait(direction, 6, c)
             value = part[z, rows, :] + rrecv[direction, 6, inner, :].astype(F32)
             out[rows, :] = (xg[z, rows, :].astype(F32) + value + dbv[...]).astype(BF16)
@@ -358,8 +375,10 @@
 ):
     lanes = np.arange(128)
     freq = np.where(lanes < ROT, 10000.0 ** (-(2.0 * (lanes // 2)) / ROT), 0.0)
-    freq = jnp.asarray(freq[None, :], dtype=F32)
-    anywhere = pl.BlockSpec(memory_space=pl.ANY)
+    steps = np.arange(GROUP)[:, None] * freq[None, :]
+    tables = np.concatenate([np.tile(freq, (8, 1)), np.cos(steps), np.sin(steps)], axis=0)
+    freq = jnp.asarray(tables, dtype=F32)
+    anywhere = pl.BlockSpec(memory_space=pltpu.HBM)
     vmem = pl.BlockSpec(memory_space=pltpu.VMEM)
     dma = pltpu.SemaphoreType.DMA
     return pl.pallas_call(
@@ -369,7 +388,7 @@
             jax.ShapeDtypeStruct((2, GROUP, HD), BF16),
             jax.ShapeDtypeStruct((2, GROUP, HD), BF16),
         ),
-        in_specs=[anywhere] * 12 + [pl.BlockSpec(memory_space=pltpu.SMEM)],
+        in_specs=[anywhere] * 13,
         out_specs=(vmem, vmem, vmem),
         scratch_shapes=[
             pltpu.VMEM((Z, TOK, COLS), BF16),
@@ -384,7 +403,7 @@
             pltpu.VMEM((1, D), F32),
             pltpu.VMEM((1, UNITS), F32),
             pltpu.VMEM((1, COLS), F32),
-            pltpu.VMEM((1, 128), F32),
+            pltpu.VMEM((8 + 2 * GROUP, 128), F32),
             pltpu.VMEM((TOK, HD), BF16),
             pltpu.VMEM((TOK, HD), BF16),
             pltpu.VMEM((TOK, HD), BF16),
@@ -393,21 +412,28 @@
             pltpu.VMEM((Z, TOK, COLS), F32),
             pltpu.VMEM((2, 7, 128, COLS), BF16),
             pltpu.VMEM((2, 7, 128, COLS), BF16),
-            dma((12,)),
+            pltpu.SMEM((2,), jnp.int32),
+            dma((13,)),
             dma((16,)),
             dma((16,)),
             dma((2, 36)),
             dma((2, 36)),
-            dma((28,)),
-            dma((28,)),
+            dma((14 * PIECES,)),
+            dma((14 * PIECES,)),
         ],
         compiler_params=pltpu.CompilerParams(
-            collective_id=0, has_side_effects=True, vmem_limit_bytes=66 * 1000 * 1000
+            collective_id=0, has_side_effects=True, vmem_limit_bytes=50 * 1000 * 1000
         ),
     )(
-        hidden_in, norm_gain[None, :], norm_shift[None, :],
-        jnp.transpose(attend_weight, (1, 0, 2)), output_weight, up_weight,
-        up_bias[None, :], down_weight, down_bias[None, :], key_cache, value_cache, freq, cached_len,
+        *[
+            pltpu.with_memory_space_constraint(v, pltpu.HBM)
+            for v in (
+                hidden_in, norm_gain[None, :], norm_shift[None, :],
+                jnp.transpose(attend_weight, (1, 0, 2)), output_weight, up_weight,
+                up_bias[None, :], down_weight, down_bias[None, :], key_cache, value_cache, freq,
+                cached_len,
+            )
+        ]
     )
 
 

time: 94.6 us -> 89.1 us (0.942)
  Pallas kernels: 89 us -> 85.9 us
  local copies, waits for them, and re-layouts: 4.8 us -> 2.01 us
    pallas_call x1, Pallas kernels: 89 us -> 85.9 us  [body(): pl.pallas_call(kernel, out_shape=(jax.ShapeDtypeStruct((TOK, COLS), BF16)...]
    unnamed x3, local copies, waits for them, and re-layouts: 4.8 us -> 2.01 us
where the time goes in v2:
time: 89.1 us; the launch traced here: 88.6 us
  Pallas kernels  85.9 us (96%)
  local copies, waits for them, and re-layouts  2.01 us (2%)
    pallas_call x1, Pallas kernels, body(): pl.pallas_call(kernel, out_shape=(jax.ShapeDtypeStruct((TOK, COLS), BF16)...  85.9 us
    unnamed x3, local copies, waits for them, and re-layouts  2.01 us

profile of v2, /device:TPU:2, one launch (start us, length us, event | category | flops | bytes accessed | tf_op | source)
XLA Modules:
  0.0 88.6 jit_solution(7864219782858234836)
XLA Ops:
  0.6 85.9 %shard_map.148 = (bf16[256,512]{1,0:T(8,128)(2,1)S(1)}, bf16[2,128,256]{2,1,0:T(8,128)(2,1)S(1)}, bf16[2,128,256]{2,1,0:T(8,128)(2,1)S(1)}) custom-call(bf16[256,512]{1,0:T(8,128)(2,1)} %hid.1, f32[1,4096]{1,0:T(1,128)} %bitcast.6, f32[1,4096]{1,0:T(1,128)} %bitcast.7, bf16[3,4096,256]{2,1,0:T(8,128)(2,1)} %bitcast.5, bf16[256,4096]{1,0:T(8,128)(2,1)} %wo.1, ...), custom_call_target="tpu_custom_call" | custom-call | tf_op jit(solution)/shard_map/pallas_call | solution.py:384
  86.6 0.7 copy.19
  87.3 0.7 copy.20
  87.9 0.7 copy.21

commit v3 on v2

--- a/solution.py
+++ b/solution.py
@@ -19,7 +19,18 @@
 COLS = D // Z
 epsilon = 1e-05
 very_low = -1e30
-PIECES = 4
+ORDER = (
+    ("Z", 1, 0), ("F", 0), ("Z", 1, 1), ("Z", 2, 0), ("Z", 2, 1), ("F", 1), ("S", 0, 0), ("Z", 3, 0),
+    ("S", 0, 2), ("Z", 3, 1), ("H", 1), ("H", 0), ("S", 0, 1), ("Z", 4, 1), ("Z", 4, 0), ("ln", 0),
+    ("S", 1, 1), ("T", 0, 0), ("ln", 1), ("project", 2), ("project", 1), ("S", 0, 3), ("S", 1, 2), ("S", 1, 3),
+    ("project", 0), ("at", 1), ("T", 0, 2), ("T", 0, 1), ("S", 1, 0), ("own", 2), ("T", 0, 3), ("at", 0),
+    ("T", 1, 1), ("P", 0), ("up", 3), ("up", 0), ("F", 2), ("T", 1, 2), ("T", 1, 3), ("T", 1, 0),
+    ("up", 2), ("up", 1), ("P", 1), ("B", 0, 0), ("N", 0, 0), ("H", 2), ("B", 0, 2), ("S", 2, 0),
+    ("B", 0, 1), ("S", 2, 1), ("N", 0, 1), ("S", 2, 2), ("S", 2, 3), ("B", 0, 3), ("T", 2, 2), ("T", 2, 1),
+    ("T", 2, 0), ("N", 0, 2), ("T", 2, 3), ("P", 2), ("B", 1, 0), ("N", 1, 0), ("N", 0, 3), ("B", 1, 1),
+    ("N", 1, 1), ("B", 0, 4), ("B", 1, 4), ("B", 1, 3), ("E", 0), ("B", 1, 2), ("N", 1, 2), ("N", 1, 3),
+    ("E", 1),
+)
 MESH = pl.DeviceIdType.MESH
 F32 = jnp.float32
 BF16 = jnp.bfloat16
@@ -30,7 +41,7 @@
     out, new_k, new_v,
     xg, nrm, wub, wdb, wqv, wov, kcv, vcv, gainv, shiftv, ubv, dbv, freqv,
     qbuf, kbuf, vbuf, ctx, act, part, rsend, rrecv, lens,
-    local_sem, zs, zr, ws, wr, ss, sr,
+    local_sem, zs, zr, ws, wr, ss, sr, xs, xr,
 ):
     r = lax.axis_index("req")
     z = lax.axis_index("head")
@@ -97,17 +108,15 @@
         if hop < zlast(direction, c):
             zsend(direction, hop + 1, c)
 
-    own = (wu, wd)
-
     def slot(w, o):
         if w == 0:
             return wub.at[pl.ds(pl.multiple_of(o * 128, 128), 128), :]
-        return wdb.at[o]
+        return wdb.at[(o // 2) * 2 + w - 1, pl.ds(pl.multiple_of((o % 2) * 512, 512), 512), :]
 
     def half(w, o, k):
         if w == 0:
             return wub.at[pl.ds(pl.multiple_of(o * 128 + 64 * k, 64), 64), :]
-        return wdb.at[o, pl.ds(512 * k, 512), :]
+        return wdb.at[(o // 2) * 2 + w - 1, pl.ds(pl.multiple_of((o % 2) * 512 + 256 * k, 256), 256), :]
 
     A_OF = (0, 3, 1, 2)
 
@@ -119,20 +128,22 @@
 
     def across(w, j, kb):
         o = device(core, a + A_OF[j], b + A_OF[kb])
-        src = own[w] if j == 0 and kb == 0 else slot(w, o)
+        src = wu if w == 0 and j == 0 and kb == 0 else slot(w, o)
         wsend(w, 20 + 4 * j + kb, src, slot(w, o), partner)
 
     def second(w, j):
         o = device(core, a + A_OF[j], b)
-        src = own[w] if j == 0 else slot(w, o)
+        src = wu if w == 0 and j == 0 else slot(w, o)
         wsend(w, 4 + 4 * j, src, slot(w, o), b_plus)
         wsend(w, 5 + 4 * j, src, slot(w, o), b_minus)
 
     def start_own(w):
-        wsend(w, 0, own[w], slot(w, r), a_plus)
-        wsend(w, 1, own[w], slot(w, r), a_minus)
+        src = wu if w == 0 else slot(w, r)
+        wsend(w, 0, src, slot(w, r), a_plus)
+        wsend(w, 1, src, slot(w, r), a_minus)
         second(w, 0)
-        across(w, 0, 0)
+        if w == 0:
+            across(w, 0, 0)
 
     def first_event(w):
         o = device(core, a + 3, b)
@@ -173,10 +184,18 @@
     def partner_waits(w):
         for j in range(4):
             for kb in range(4):
+                if w > 0 and j == 0 and kb == 0:
+                    continue
                 o = device(1 - core, b + A_OF[j], a + A_OF[kb])
                 wwait(w, 20 + 4 * j + kb, slot(w, o))
 
     locals_ = []
+    pending = {}
+
+    def need(*names):
+        for name in names:
+            if name in pending:
+                pending.pop(name).wait()
 
     def bring(src, dst):
         copy = pltpu.make_async_copy(src, dst, local_sem.at[len(locals_)])
@@ -188,17 +207,20 @@
         zsend(0, 1, c)
         zsend(1, 1, c)
     start_own(0)
-    start_own(1)
-    c_x = bring(hid, xg.at[z])
+    launch(wd, wdb.at[r], xs.at[0], xr.at[0], (partner, z))
+    c_d = bring(wd, wdb.at[r])
+    pending["x"] = bring(hid, xg.at[z])
     c_small = [bring(lens_in, lens), bring(gain, gainv), bring(shift, shiftv), bring(ub, ubv), bring(db, dbv), bring(freq, freqv)]
-    c_u = bring(wu, slot(0, r))
-    c_d = bring(wd, slot(1, r))
-    c_q = bring(wq, wqv)
-    c_k = bring(kc, kcv)
-    c_v = bring(vc, vcv)
-    c_o = bring(wo, wov)
+    pending["u"] = bring(wu, slot(0, r))
+    pending["q"] = bring(wq, wqv)
+    pending["k"] = bring(kc, kcv)
+    pending["v"] = bring(vc, vcv)
+    pending["o"] = bring(wo, wov)
     for copy in c_small:
         copy.wait()
+    c_d.wait()
+    remote(wdb.at[partner], wdb.at[partner], xs.at[0], xr.at[0], (partner, z)).wait_recv()
+    start_own(1)
 
     lane = lax.broadcasted_iota(jnp.int32, (TOK, 128), 1)
     turn = [lens[q].astype(F32) * freqv[pl.ds(0, 8), :] for q in range(2)]
@@ -214,68 +236,47 @@
         sine = jnp.concatenate(sines, axis=0)
         return cosine, jnp.where(lane % 2 == 0, -sine, sine)
 
-    def rotate(t):
+    def rotate(t, cosine, sine):
         head = t[:, :128]
         swapped = jnp.where(lane % 2 == 0, pltpu.roll(head, 127, 1), pltpu.roll(head, 1, 1))
         return jnp.concatenate([head * cosine + swapped * sine, t[:, 128:]], axis=1)
 
-    zevent(0, 1, 0), zevent(1, 1, 0)
-    first_event(0)
-    second_event(0, 0)
-    zevent(0, 1, 1), zevent(1, 1, 1)
-    zevent(0, 2, 0), zevent(1, 2, 0)
-    zevent(0, 2, 1), zevent(1, 2, 1)
-    first_event(1)
-    second_event(1, 0)
-    zevent(0, 3, 0), zevent(1, 3, 0)
-    first_halves(0)
-    second_halves(0, 0)
-    zevent(0, 3, 1), zevent(1, 3, 1)
-    second_event(0, 1)
-    second_event(0, 2)
-    zevent(0, 4, 0), zevent(1, 4, 1)
-    c_x.wait()
-
-    @pl.loop(0, TOK // 16)
-    def _(i):
-        rows = pl.ds(pl.multiple_of(i * 16, 16), 16)
-        total = jnp.zeros((16, 1), F32)
-        for h in range(Z):
-            total += jnp.sum(xg[h, rows, :].astype(F32), axis=1, keepdims=True)
-        mean = total * (1.0 / D)
-        square = jnp.zeros((16, 1), F32)
-        for h in range(Z):
-            center = xg[h, rows, :].astype(F32) - mean
-            square += jnp.sum(center * center, axis=1, keepdims=True)
-        scale = lax.rsqrt(square * (1.0 / D) + epsilon)
-        for h in range(Z):
-            cols = slice(h * COLS, (h + 1) * COLS)
-            center = xg[h, rows, :].astype(F32) - mean
-            nrm[rows, cols] = (center * scale * gainv[:, cols] + shiftv[:, cols]).astype(BF16)
-
-    first_halves(1)
-    second_halves(1, 0)
-    second_event(0, 3)
-
-    cosine, sine = rotation()
-    c_q.wait()
-    qbuf[...] = rotate(jnp.dot(nrm[...], wqv[0], preferred_element_type=F32)).astype(BF16)
-    second_halves(0, 1)
-    second_halves(0, 2)
-    kbuf[...] = rotate(jnp.dot(nrm[...], wqv[1], preferred_element_type=F32)).astype(BF16)
-    vbuf[...] = jnp.dot(nrm[...], wqv[2], preferred_element_type=F32).astype(BF16)
-    second_event(1, 1)
-    second_event(1, 2)
-    second_halves(0, 3)
-    for q in range(2):
-        new_k[q] = kbuf[pl.ds(q * GROUP, GROUP), :]
-        new_v[q] = vbuf[pl.ds(q * GROUP, GROUP), :]
-
-    c_k.wait()
-    c_v.wait()
+    def norm(n):
+        need("x")
+
+        @pl.loop(n * 8, n * 8 + 8)
+        def _(i):
+            rows = pl.ds(pl.multiple_of(i * 16, 16), 16)
+            total = jnp.zeros((16, 1), F32)
+            for h in range(Z):
+                total += jnp.sum(xg[h, rows, :].astype(F32), axis=1, keepdims=True)
+            mean = total * (1.0 / D)
+            square = jnp.zeros((16, 1), F32)
+            for h in range(Z):
+                center = xg[h, rows, :].astype(F32) - mean
+                square += jnp.sum(center * center, axis=1, keepdims=True)
+            scale = lax.rsqrt(square * (1.0 / D) + epsilon)
+            for h in range(Z):
+                cols = slice(h * COLS, (h + 1) * COLS)
+                center = xg[h, rows, :].astype(F32) - mean
+                nrm[rows, cols] = (center * scale * gainv[:, cols] + shiftv[:, cols]).astype(BF16)
+
+    def project(n):
+        need("q")
+        value = jnp.dot(nrm[...], wqv[n], preferred_element_type=F32)
+        if n < 2:
+            value = rotate(value, *rotation())
+        buffer = (qbuf, kbuf, vbuf)[n]
+        buffer[...] = value.astype(BF16)
+        if n > 0:
+            given = (new_k, new_v)[n - 1]
+            for q in range(2):
+                given[q] = buffer[pl.ds(q * GROUP, GROUP), :]
+
     nt = (((1,), (1,)), ((), ()))
 
     def attend(q):
+        need("k", "v")
         rows = pl.ds(q * GROUP, GROUP)
         query = qbuf[rows, :]
         old = lax.dot_general(query, kcv[q], nt, preferred_element_type=F32) * (HD ** -0.5)
@@ -293,78 +294,81 @@
         mixed += jnp.dot(fresh.astype(BF16), vbuf[rows, :], preferred_element_type=F32)
         ctx[rows, :] = (mixed / total).astype(BF16)
 
-    attend(0)
-    second_event(1, 3)
-    attend(1)
-
-    c_u.wait()
-    partner_waits(0)
-
-    @pl.loop(0, UNITS // 256)
-    def _(n):
-        cols = pl.ds(pl.multiple_of(n * 256, 256), 256)
+
+    def feed(n):
+        need("u")
+        cols = slice(n * 256, n * 256 + 256)
         upward = jnp.dot(nrm[...], wub[:, cols], preferred_element_type=F32) + ubv[:, cols]
         act[:, cols] = jax.nn.gelu(upward, approximate=True).astype(BF16)
 
-    second_halves(1, 1)
-    second_halves(1, 2)
-    second_halves(1, 3)
-    c_d.wait()
-    c_o.wait()
-    partner_waits(1)
-
-    def block(t):
-        for i in range(2):
-            weight = jnp.concatenate([wdb[4 * t + 2 * i], wdb[4 * t + 2 * i + 1]], axis=1)
-            cols = pl.ds(pl.multiple_of(t * COLS + 256 * i, 256), 256)
-            part[t, :, 256 * i:256 * (i + 1)] = jnp.dot(
-                act[...], weight, preferred_element_type=F32
-            ) + jnp.dot(ctx[...], wov[:, cols], preferred_element_type=F32)
-
-    piece = GROUP // PIECES
-
-    def rwait(direction, s, c):
-        k = (direction * 7 + s) * PIECES + c
-        view = rrecv.at[direction, s, pl.ds(piece * c, piece), :]
-        remote(view, view, ss.at[k], sr.at[k], (r, z_plus)).wait_recv()
-
-    def hand_on(direction, s):
-        t = (z + 7 - s) % Z if direction == 0 else (z + 1 + s) % Z
-        for c in range(PIECES):
-            rows = pl.ds(128 * direction + piece * c, piece)
-            inner = pl.ds(piece * c, piece)
-            value = part[t, rows, :]
-            if s > 0:
-                rwait(direction, s - 1, c)
-                value += rrecv[direction, s - 1, inner, :].astype(F32)
-            rsend[direction, s, inner, :] = value.astype(BF16)
-            k = (direction * 7 + s) * PIECES + c
-            launch(
-                rsend.at[direction, s, inner, :], rrecv.at[direction, s, inner, :],
-                ss.at[k], sr.at[k], (r, z_plus if direction == 0 else z_minus),
-            )
-
-    block((z + 7) % Z)
-    hand_on(0, 0)
-    block((z + 1) % Z)
-    hand_on(1, 0)
-    for s in range(1, 7):
-        if s < 3:
-            block((z + 7 - s) % Z)
-            block((z + 1 + s) % Z)
-        elif s == 3:
-            block((z + 4) % Z)
-        elif s == 4:
-            block(z)
-        hand_on(0, s)
-        hand_on(1, s)
-    for c in range(PIECES):
+    def block(g, t):
+        o = 4 * t + g
+        weight = jnp.concatenate([wdb[o], wdb[o + 2]], axis=1)
+        cols = [pl.ds(pl.multiple_of((o + 2 * i) * 128, 128), 128) for i in range(2)]
+        last = jnp.concatenate([wov[:, cols[0]], wov[:, cols[1]]], axis=1)
+        part[g, t] = jnp.dot(act[...], weight, preferred_element_type=F32) + jnp.dot(
+            ctx[...], last, preferred_element_type=F32
+        )
+
+    def hop(g, direction, s, c):
+        k = ((g * 2 + direction) * 4 + s) * 4 + c
+        rows = pl.ds(64 * c, 64)
+        return remote(
+            rsend.at[g, direction, s, rows, :], rrecv.at[g, direction, s, rows, :],
+            ss.at[k], sr.at[k], (r, z_plus if direction == 0 else z_minus),
+        )
+
+    def pieces(direction, s):
+        return range(4) if s > 0 else range(2 * direction, 2 * direction + 2)
+
+    def hand_on(g, s):
+        for c in (0, 1, 2, 3):
+            rows = pl.ds(64 * c, 64)
+            for direction in range(2):
+                if c not in pieces(direction, s):
+                    continue
+                t = (z + 4 - s) % Z if direction == 0 else (z + 4 + s) % Z
+                value = part[g, t, rows, :]
+                if s > 0 and c in pieces(direction, s - 1):
+                    hop(g, direction, s - 1, c).wait_recv()
+                    value += rrecv[g, direction, s - 1, rows, :].astype(F32)
+                rsend[g, direction, s, rows, :] = value.astype(BF16)
+                copy = hop(g, direction, s, c)
+                copy.start()
+                sent.append(copy)
+
+    def finish(g):
+        for c in range(4):
+            rows = pl.ds(64 * c, 64)
+            total = part[g, z, rows, :]
+            for direction in range(2):
+                hop(g, direction, 3, c).wait_recv()
+                total += rrecv[g, direction, 3, rows, :].astype(F32)
+            for i in range(2):
+                cols = slice(256 * i + 128 * g, 256 * i + 128 * g + 128)
+                mine = xg[z, rows, cols].astype(F32)
+                out[rows, cols] = (mine + total[:, 128 * i:128 * (i + 1)] + dbv[:, cols]).astype(BF16)
+
+    def blocks(g, s):
+        need("o")
+        if s in (0, 4):
+            block(g, (z + 4 - s) % Z)
+        else:
+            block(g, (z + 4 - s) % Z)
+            block(g, (z + 4 + s) % Z)
+
+    def both(distance, c):
         for direction in range(2):
-            rows = pl.ds(128 * direction + piece * c, piece)
-            inner = pl.ds(piece * c, piece)
-            rwait(direction, 6, c)
-            value = part[z, rows, :] + rrecv[direction, 6, inner, :].astype(F32)
-            out[rows, :] = (xg[z, rows, :].astype(F32) + value + dbv[...]).astype(BF16)
+            if distance <= zlast(direction, c):
+                zevent(direction, distance, c)
+
+    steps = {
+        "Z": both, "F": first_event, "H": first_halves, "S": second_event, "T": second_halves,
+        "P": partner_waits, "B": blocks, "N": hand_on, "E": finish, "own": start_own,
+        "ln": norm, "project": project, "at": attend, "up": feed,
+    }
+    for step in ORDER:
+        steps[step[0]](*step[1:])
     for copy in sent:
         copy.wait_send()
 
@@ -409,17 +413,19 @@
             pltpu.VMEM((TOK, HD), BF16),
             pltpu.VMEM((TOK, HD), BF16),
             pltpu.VMEM((TOK, UNITS), BF16),
-            pltpu.VMEM((Z, TOK, COLS), F32),
-            pltpu.VMEM((2, 7, 128, COLS), BF16),
-            pltpu.VMEM((2, 7, 128, COLS), BF16),
+            pltpu.VMEM((2, Z, TOK, 256), F32),
+            pltpu.VMEM((2, 2, 4, TOK, 256), BF16),
+            pltpu.VMEM((2, 2, 4, TOK, 256), BF16),
             pltpu.SMEM((2,), jnp.int32),
             dma((13,)),
             dma((16,)),
             dma((16,)),
-            dma((2, 36)),
-            dma((2, 36)),
-            dma((14 * PIECES,)),
-            dma((14 * PIECES,)),
+            dma((3, 36)),
+            dma((3, 36)),
+            dma((64,)),
+            dma((64,)),
+            dma((1,)),
+            dma((1,)),
         ],
         compiler_params=pltpu.CompilerParams(
             collective_id=0, has_side_effects=True, vmem_limit_bytes=50 * 1000 * 1000

time: 89.1 us -> 82.2 us (0.923)
  Pallas kernels: 85.9 us -> 78.4 us
    pallas_call x1, Pallas kernels: 85.9 us -> 78.4 us  [body(): pl.pallas_call(kernel, out_shape=(jax.ShapeDtypeStruct((TOK, COLS), BF16)...]
where the time goes in v3:
time: 82.2 us; the launch traced here: 81 us
  Pallas kernels  78.4 us (95%)
  local copies, waits for them, and re-layouts  2.01 us (2%)
    pallas_call x1, Pallas kernels, body(): pl.pallas_call(kernel, out_shape=(jax.ShapeDtypeStruct((TOK, COLS), BF16)...  78.4 us
    unnamed x3, local copies, waits for them, and re-layouts  2.01 us

profile of v3, /device:TPU:2, one launch (start us, length us, event | category | flops | bytes accessed | tf_op | source)
XLA Modules:
  0.0 81.0 jit_solution(2409700332277504230)
XLA Ops:
  0.6 78.4 %shard_map.148 = (bf16[256,512]{1,0:T(8,128)(2,1)S(1)}, bf16[2,128,256]{2,1,0:T(8,128)(2,1)S(1)}, bf16[2,128,256]{2,1,0:T(8,128)(2,1)S(1)}) custom-call(bf16[256,512]{1,0:T(8,128)(2,1)} %hid.1, f32[1,4096]{1,0:T(1,128)} %bitcast.6, f32[1,4096]{1,0:T(1,128)} %bitcast.7, bf16[3,4096,256]{2,1,0:T(8,128)(2,1)} %bitcast.5, bf16[256,4096]{1,0:T(8,128)(2,1)} %wo.1, ...), custom_call_target="tpu_custom_call" | custom-call | tf_op jit(solution)/shard_map/pallas_call | solution.py:388
  79.0 0.7 copy.19
  79.7 0.7 copy.20
  80.4 0.7 copy.21

commit v4 on v3

--- a/solution.py
+++ b/solution.py
@@ -20,15 +20,15 @@
 epsilon = 1e-05
 very_low = -1e30
 ORDER = (
-    ("Z", 1, 0), ("F", 0), ("Z", 1, 1), ("Z", 2, 0), ("Z", 2, 1), ("F", 1), ("S", 0, 0), ("Z", 3, 0),
-    ("S", 0, 2), ("Z", 3, 1), ("H", 1), ("H", 0), ("S", 0, 1), ("Z", 4, 1), ("Z", 4, 0), ("ln", 0),
-    ("S", 1, 1), ("T", 0, 0), ("ln", 1), ("project", 2), ("project", 1), ("S", 0, 3), ("S", 1, 2), ("S", 1, 3),
-    ("project", 0), ("at", 1), ("T", 0, 2), ("T", 0, 1), ("S", 1, 0), ("own", 2), ("T", 0, 3), ("at", 0),
-    ("T", 1, 1), ("P", 0), ("up", 3), ("up", 0), ("F", 2), ("T", 1, 2), ("T", 1, 3), ("T", 1, 0),
-    ("up", 2), ("up", 1), ("P", 1), ("B", 0, 0), ("N", 0, 0), ("H", 2), ("B", 0, 2), ("S", 2, 0),
-    ("B", 0, 1), ("S", 2, 1), ("N", 0, 1), ("S", 2, 2), ("S", 2, 3), ("B", 0, 3), ("T", 2, 2), ("T", 2, 1),
-    ("T", 2, 0), ("N", 0, 2), ("T", 2, 3), ("P", 2), ("B", 1, 0), ("N", 1, 0), ("N", 0, 3), ("B", 1, 1),
-    ("N", 1, 1), ("B", 0, 4), ("B", 1, 4), ("B", 1, 3), ("E", 0), ("B", 1, 2), ("N", 1, 2), ("N", 1, 3),
+    ("Z", 1, 0), ("F", 0), ("S", 0, 0), ("Z", 1, 1), ("F", 1), ("Z", 2, 0), ("H", 0), ("Z", 2, 1),
+    ("S", 0, 1), ("H", 1), ("S", 0, 2), ("Z", 3, 0), ("Z", 3, 1), ("S", 1, 2), ("T", 0, 0), ("S", 1, 1),
+    ("Z", 4, 1), ("Z", 4, 0), ("ln", 0), ("S", 0, 3), ("S", 1, 0), ("ln", 1), ("T", 0, 1), ("project", 2),
+    ("S", 1, 3), ("project", 1), ("project", 0), ("T", 1, 2), ("T", 0, 2), ("at", 1), ("T", 1, 1), ("own", 2),
+    ("T", 1, 0), ("T", 0, 3), ("at", 0), ("T", 1, 3), ("P", 0), ("up", 3), ("up", 0), ("S", 2, 0),
+    ("F", 2), ("up", 2), ("up", 1), ("P", 1), ("B", 0, 0), ("N", 0, 0), ("T", 2, 0), ("H", 2),
+    ("B", 0, 2), ("B", 0, 1), ("S", 2, 1), ("N", 0, 1), ("S", 2, 2), ("S", 2, 3), ("T", 2, 1), ("B", 0, 3),
+    ("T", 2, 2), ("N", 0, 2), ("T", 2, 3), ("P", 2), ("B", 1, 0), ("N", 1, 0), ("N", 0, 3), ("B", 1, 1),
+    ("N", 1, 1), ("B", 1, 2), ("B", 0, 4), ("B", 1, 4), ("E", 0), ("N", 1, 2), ("B", 1, 3), ("N", 1, 3),
     ("E", 1),
 )
 MESH = pl.DeviceIdType.MESH

time: 82.2 us -> 81.1 us (0.987)
  Pallas kernels: 78.4 us -> 77.2 us
    pallas_call x1, Pallas kernels: 78.4 us -> 77.2 us  [body(): pl.pallas_call(kernel, out_shape=(jax.ShapeDtypeStruct((TOK, COLS), BF16)...]
where the time goes in v4:
time: 81.1 us; the launch traced here: 79.9 us
  Pallas kernels  77.2 us (95%)
  local copies, waits for them, and re-layouts  2.01 us (2%)
    pallas_call x1, Pallas kernels, body(): pl.pallas_call(kernel, out_shape=(jax.ShapeDtypeStruct((TOK, COLS), BF16)...  77.2 us
    unnamed x3, local copies, waits for them, and re-layouts  2.01 us

profile of v4, /device:TPU:2, one launch (start us, length us, event | category | flops | bytes accessed | tf_op | source)
XLA Modules:
  0.0 79.9 jit_solution(17872938436935790527)
XLA Ops:
  0.6 77.2 %shard_map.148 = (bf16[256,512]{1,0:T(8,128)(2,1)S(1)}, bf16[2,128,256]{2,1,0:T(8,128)(2,1)S(1)}, bf16[2,128,256]{2,1,0:T(8,128)(2,1)S(1)}) custom-call(bf16[256,512]{1,0:T(8,128)(2,1)} %hid.1, f32[1,4096]{1,0:T(1,128)} %bitcast.6, f32[1,4096]{1,0:T(1,128)} %bitcast.7, bf16[3,4096,256]{2,1,0:T(8,128)(2,1)} %bitcast.5, bf16[256,4096]{1,0:T(8,128)(2,1)} %wo.1, ...), custom_call_target="tpu_custom_call" | custom-call | tf_op jit(solution)/shard_map/pallas_call | solution.py:388
  77.9 0.7 copy.19
  78.6 0.7 copy.20
  79.2 0.7 copy.21

commit v5 on v4

--- a/solution.py
+++ b/solution.py
@@ -23,7 +23,7 @@
     ("Z", 1, 0), ("F", 0), ("S", 0, 0), ("Z", 1, 1), ("F", 1), ("Z", 2, 0), ("H", 0), ("Z", 2, 1),
     ("S", 0, 1), ("H", 1), ("S", 0, 2), ("Z", 3, 0), ("Z", 3, 1), ("S", 1, 2), ("T", 0, 0), ("S", 1, 1),
     ("Z", 4, 1), ("Z", 4, 0), ("ln", 0), ("S", 0, 3), ("S", 1, 0), ("ln", 1), ("T", 0, 1), ("project", 2),
-    ("S", 1, 3), ("project", 1), ("project", 0), ("T", 1, 2), ("T", 0, 2), ("at", 1), ("T", 1, 1), ("own", 2),
+    ("S", 1, 3), ("own", 2), ("project", 1), ("project", 0), ("T", 1, 2), ("T", 0, 2), ("at", 1), ("T", 1, 1),
     ("T", 1, 0), ("T", 0, 3), ("at", 0), ("T", 1, 3), ("P", 0), ("up", 3), ("up", 0), ("S", 2, 0),
     ("F", 2), ("up", 2), ("up", 1), ("P", 1), ("B", 0, 0), ("N", 0, 0), ("T", 2, 0), ("H", 2),
     ("B", 0, 2), ("B", 0, 1), ("S", 2, 1), ("N", 0, 1), ("S", 2, 2), ("S", 2, 3), ("T", 2, 1), ("B", 0, 3),

time: 81.1 us -> 82 us (1.011)
  Pallas kernels: 77.2 us -> 78.2 us
    pallas_call x1, Pallas kernels: 77.2 us -> 78.2 us  [body(): pl.pallas_call(kernel, out_shape=(jax.ShapeDtypeStruct((TOK, COLS), BF16)...]
where the time goes in v5:
time: 82 us; the launch traced here: 80.8 us
  Pallas kernels  78.2 us (95%)
  local copies, waits for them, and re-layouts  2.01 us (2%)
    pallas_call x1, Pallas kernels, body(): pl.pallas_call(kernel, out_shape=(jax.ShapeDtypeStruct((TOK, COLS), BF16)...  78.2 us
    unnamed x3, local copies, waits for them, and re-layouts  2.01 us

profile of v5, /device:TPU:2, one launch (start us, length us, event | category | flops | bytes accessed | tf_op | source)
XLA Modules:
  0.0 80.8 jit_solution(1741122028518408786)
XLA Ops:
  0.6 78.2 %shard_map.148 = (bf16[256,512]{1,0:T(8,128)(2,1)S(1)}, bf16[2,128,256]{2,1,0:T(8,128)(2,1)S(1)}, bf16[2,128,256]{2,1,0:T(8,128)(2,1)S(1)}) custom-call(bf16[256,512]{1,0:T(8,128)(2,1)} %hid.1, f32[1,4096]{1,0:T(1,128)} %bitcast.6, f32[1,4096]{1,0:T(1,128)} %bitcast.7, bf16[3,4096,256]{2,1,0:T(8,128)(2,1)} %bitcast.5, bf16[256,4096]{1,0:T(8,128)(2,1)} %wo.1, ...), custom_call_target="tpu_custom_call" | custom-call | tf_op jit(solution)/shard_map/pallas_call | solution.py:388
  78.8 0.7 copy.19
  79.5 0.7 copy.20
  80.2 0.7 copy.21
